TPU v7x, 128 devices: a whole 4x4x4 slice. The times are simulated.
128 devices in a mesh: corpus: 32 (over y, z, core), query: 4 (over x).
Axes of the slice: x: 4, y: 4, z: 4, core: 2. Of those that a mesh axis runs over, the one named last changes fastest.
Arguments:
- queries: bfloat16 [32768, 768], P(('corpus', 'query')), may hold values from -8 to 8
- probes: int32 [32768, 4], P(('corpus', 'query')), may hold values from 0 to 1023, as said below
- targets: int32 [32768, 8], P(('corpus', 'query')), may hold values from 0 to 4095, all different within a row
- passage_codes: int32 [1024, 96, 1024], P('corpus'), may hold values from 0 to 15
- codebook: float32 [16, 768], replicated, may hold values from -6 to 6
Outputs:
- grad_queries: bfloat16 [32768, 768], P(('corpus', 'query'))
- codebook_step: float32 [16, 768], replicated
Inputs may be any that keep to these rules, and one draw needn't show every extreme that they name: `probes`: each row names 4 different lists; list l belongs to index l // 32 of corpus. In every aligned block of 256 rows (the rows of one device) no list is named more than 2 times, and one list, the same one in every block, is named exactly 2 times. `targets`: each row names 8 different candidates; column r holds the candidate of rank r.
All inputs are finite; a program needn't handle non-finite values.
Results may differ from a plain program's by a relative error of at most 0.01.
The roundings to bfloat16 on the way count: a program that leaves them out, or rounds other values in their place, can miss the bound.
Values may be sent and summed in bfloat16 or wider, within the bound.
No kernel may reach another device: no remote copies, remote signals or barrier semaphores. Data moves between devices by JAX's collectives and lax.ppermute only.
A program may use at most 192 MiB of HBM per device.

v0:
```python
import jax
import jax.numpy as jnp
from jax import lax
from jax.sharding import PartitionSpec as P

D = 768
SUBSPACES = 96
CENTROIDS = 16
SUBDIM = 8
PASSAGES = 1024
PROBES = 4
TARGETS = 8
NEGATIVE = -1e30
EPSILON = 1e-06


def rank_weights():
    levels = jnp.arange(TARGETS, dtype=jnp.int32).astype(jnp.float32)
    return 2.0 * (TARGETS - levels) / (TARGETS * (TARGETS + 1.0))


def rank_slots(list_keys, key_count, keep):
    key_ids = jnp.arange(key_count, dtype=jnp.int32)
    marked = ((list_keys[:, None] == key_ids[None, :]) & keep[:, None]).astype(jnp.int32)
    running = jnp.cumsum(marked, axis=0)
    return jnp.sum(marked * running, axis=1) - 1


def note_block(probes, targets):
    row_count = probes.shape[0]
    probe_cols = jnp.arange(PROBES, dtype=jnp.int32)
    inside = targets[:, None, :] // PASSAGES == probe_cols[None, :, None]
    target_spot = jnp.where(inside, targets[:, None, :] % PASSAGES, -1)
    query_ids = jnp.broadcast_to(
        jnp.arange(row_count, dtype=jnp.int32)[:, None, None], (row_count, PROBES, 1)
    )
    return jnp.concatenate([query_ids, target_spot], axis=2).reshape(
        row_count * PROBES, TARGETS + 1
    )


def lookup_rows(rows_block, codebook):
    lead_shape = rows_block.shape[:-1]
    split_rows = rows_block.astype(jnp.float32).reshape(lead_shape + (SUBSPACES, SUBDIM))
    centroids = codebook.reshape(CENTROIDS, SUBSPACES, SUBDIM)
    lut_rows = jnp.einsum(
        "...me,kme->...mk", split_rows, centroids, precision=lax.Precision.HIGHEST
    )
    return lut_rows.reshape(lead_shape + (SUBSPACES * CENTROIDS,)).astype(jnp.bfloat16)


def code_one_hot(code_block):
    levels = jnp.arange(CENTROIDS, dtype=jnp.int32)
    marked = code_block[:, :, None, :] == levels[None, None, :, None]
    return marked.astype(jnp.bfloat16).reshape(
        code_block.shape[0], SUBSPACES * CENTROIDS, code_block.shape[2]
    )


def group_size(lists_dev, slot_rows):
    group_width = 1
    while (
        group_width * 2 <= lists_dev
        and lists_dev % (group_width * 2) == 0
        and (group_width * slot_rows < 512)
    ):
        group_width = group_width * 2
    return group_width


def first_pass(got_rows, passage_codes, codebook, group_width):
    lists_dev, slot_rows = (got_rows.shape[0], got_rows.shape[1])
    groups = lists_dev // group_width

    def score_piece(pieces):
        row_group, code_group = pieces
        lut_rows = lookup_rows(row_group, codebook)
        one_hot = code_one_hot(code_group)
        scores = jnp.einsum("grk,gkl->grl", lut_rows, one_hot, preferred_element_type=jnp.float32)
        top_score = jnp.max(scores, axis=2)
        exp_total = jnp.sum(jnp.exp(scores - top_score[:, :, None]), axis=2)
        return (scores, top_score, exp_total)

    scores, top_score, exp_total = lax.map(
        score_piece,
        (
            got_rows.reshape(groups, group_width, slot_rows, D),
            passage_codes.reshape(groups, group_width, SUBSPACES, PASSAGES),
        ),
    )
    return (
        scores.reshape(lists_dev, slot_rows, PASSAGES),
        top_score.reshape(lists_dev, slot_rows),
        exp_total.reshape(lists_dev, slot_rows),
    )


def second_pass(
    got_rows, got_notes, passage_codes, codebook, scores, query_top, query_total, group_width
):
    lists_dev, slot_rows = (got_rows.shape[0], got_rows.shape[1])
    groups = lists_dev // group_width
    weights = rank_weights()
    places = jnp.arange(PASSAGES, dtype=jnp.int32)
    centroids = codebook.reshape(CENTROIDS, SUBSPACES, SUBDIM)
    highest = lax.Precision.HIGHEST

    def grad_piece(pieces):
        row_group, note_group, code_group, score_group, top_group, total_group = pieces
        one_hot = code_one_hot(code_group)
        target_spot = note_group[:, :, 1:]
        teacher = jnp.sum(
            jnp.where(target_spot[:, :, :, None] == places, weights[:, None], 0.0), axis=2
        )
        student = jnp.exp(score_group - top_group[:, :, None]) / total_group[:, :, None]
        is_valid = note_group[:, :, 0] >= 0
        grad_scores = jnp.where(is_valid[:, :, None], student - teacher, 0.0).astype(jnp.bfloat16)
        histogram = jnp.einsum(
            "grl,gkl->grk", grad_scores, one_hot, preferred_element_type=jnp.float32
        )
        histogram = histogram.reshape(group_width, slot_rows, SUBSPACES, CENTROIDS)
        partial_value = jnp.einsum("grmk,kme->grme", histogram, centroids, precision=highest)
        split_rows = row_group.astype(jnp.float32).reshape(
            group_width, slot_rows, SUBSPACES, SUBDIM
        )
        book_part = jnp.einsum("grmk,grme->kme", histogram, split_rows, precision=highest)
        return (partial_value.reshape(group_width, slot_rows, D), book_part)

    partial_value, book_part = lax.map(
        grad_piece,
        (
            got_rows.reshape(groups, group_width, slot_rows, D),
            got_notes.reshape(groups, group_width, slot_rows, TARGETS + 1),
            passage_codes.reshape(groups, group_width, SUBSPACES, PASSAGES),
            scores.reshape(groups, group_width, slot_rows, PASSAGES),
            query_top.reshape(groups, group_width, slot_rows),
            query_total.reshape(groups, group_width, slot_rows),
        ),
    )
    return (
        partial_value.reshape(lists_dev, slot_rows, D),
        jnp.sum(book_part, axis=0).reshape(CENTROIDS, D),
    )


def shards(queries, probes, targets, passage_codes, codebook):
    corpus_size = lax.axis_size("corpus")
    query_rows = queries.shape[0]
    lists_dev = passage_codes.shape[0]
    list_total = lists_dev * corpus_size
    capacity = min(query_rows, max(2, 2 * PROBES * query_rows // list_total))
    slot_rows = corpus_size * capacity
    slot_count = lists_dev * slot_rows
    group_width = group_size(lists_dev, slot_rows)
    flat_probes = probes.reshape(-1)
    local_list = flat_probes % lists_dev
    owner_ids = flat_probes // lists_dev
    slot_rank = rank_slots(flat_probes, list_total, jnp.ones(flat_probes.shape, jnp.bool_))
    note_rows = note_block(probes, targets)
    placed = (local_list * corpus_size + owner_ids) * capacity + slot_rank
    sending = (
        jnp.zeros((slot_count, D), jnp.bfloat16).at[placed].set(jnp.repeat(queries, PROBES, axis=0))
    )
    note_buffer = jnp.full((slot_count, TARGETS + 1), -1, jnp.int32).at[placed].set(note_rows)
    got_rows, got_notes = (
        lax.all_to_all(
            sending.reshape(lists_dev, corpus_size, capacity, D),
            "corpus",
            split_axis=1,
            concat_axis=1,
            tiled=True,
        ),
        lax.all_to_all(
            note_buffer.reshape(lists_dev, corpus_size, capacity, TARGETS + 1),
            "corpus",
            split_axis=1,
            concat_axis=1,
            tiled=True,
        ),
    )
    got_rows = got_rows.reshape(lists_dev, slot_rows, D)
    got_notes = got_notes.reshape(lists_dev, slot_rows, TARGETS + 1)
    is_valid = got_notes[:, :, 0] >= 0
    scores, top_score, exp_total = first_pass(got_rows, passage_codes, codebook, group_width)
    top_score = jnp.where(is_valid, top_score, NEGATIVE)
    exp_total = jnp.where(is_valid, exp_total, 0.0)
    back_top, back_total = (
        lax.all_to_all(
            top_score.reshape(lists_dev, corpus_size, capacity),
            "corpus",
            split_axis=1,
            concat_axis=1,
            tiled=True,
        ),
        lax.all_to_all(
            exp_total.reshape(lists_dev, corpus_size, capacity),
            "corpus",
            split_axis=1,
            concat_axis=1,
            tiled=True,
        ),
    )
    entry_top = back_top.reshape(-1)[placed].reshape(query_rows, PROBES)
    entry_total = back_total.reshape(-1)[placed].reshape(query_rows, PROBES)
    own_top = jnp.max(entry_top, axis=1)
    own_total = jnp.sum(entry_total * jnp.exp(entry_top - own_top[:, None]), axis=1)
    slot_top = jnp.zeros((slot_count,), jnp.float32).at[placed].set(jnp.repeat(own_top, PROBES))
    slot_total = jnp.ones((slot_count,), jnp.float32).at[placed].set(jnp.repeat(own_total, PROBES))
    query_top, query_total = (
        lax.all_to_all(
            slot_top.reshape(lists_dev, corpus_size, capacity),
            "corpus",
            split_axis=1,
            concat_axis=1,
            tiled=True,
        ),
        lax.all_to_all(
            slot_total.reshape(lists_dev, corpus_size, capacity),
            "corpus",
            split_axis=1,
            concat_axis=1,
            tiled=True,
        ),
    )
    query_top = query_top.reshape(lists_dev, slot_rows)
    query_total = query_total.reshape(lists_dev, slot_rows)
    query_top = jnp.where(is_valid, query_top, 0.0)
    query_total = jnp.where(is_valid, query_total, 1.0)
    partial_value, book_part = second_pass(
        got_rows, got_notes, passage_codes, codebook, scores, query_top, query_total, group_width
    )
    returned = lax.all_to_all(
        partial_value.reshape(lists_dev, corpus_size, capacity, D),
        "corpus",
        split_axis=1,
        concat_axis=1,
        tiled=True,
    )
    per_probe = returned.reshape(slot_count, D)[placed].reshape(query_rows, PROBES, D)
    grad_queries = jnp.sum(per_probe, axis=1)
    book_sum = lax.psum(book_part, ("corpus", "query"))
    normed = book_sum * lax.rsqrt(jnp.mean(book_sum * book_sum) + EPSILON)
    return (grad_queries.astype(jnp.bfloat16), normed)


def solution(mesh):
    placed = (
        P(("corpus", "query"), None),
        P(("corpus", "query"), None),
        P(("corpus", "query"), None),
        P("corpus", None, None),
        P(),
    )
    return jax.shard_map(
        shards,
        mesh=mesh,
        in_specs=placed,
        out_specs=(P(("corpus", "query"), None), P()),
        check_vma=False,
    )
```

profile of v0, /device:TPU:1, one launch (start us, length us, event | category | flops | bytes accessed | tf_op | source)
XLA Modules:
  0.0 697.2 jit_solution(16750538512104853884)
XLA Ops:
  4.4 2.6 broadcast_add_fusion
  7.0 2.4 copy.130
  11.3 3.6 scatter_custom_fusion
  16.7 9.6 %all-to-all-start = ((s32[32,1,576]{2,1,0:T(1,128)}), s32[32,1,576]{2,1,0:T(1,128)S(1)}, u32[]{:S(2)}, u32[]{:S(2)}) async-start(s32[32,1,576]{2,1,0:T(1,128)} %reshape.393), calls=%async_computation | async-start | bytes 163840 | tf_op jit(solution)/shard_map/all_to_all | solution.py:173
  28.1 7.1 %scatter_custom_fusion.1 = bf16[2048,768]{1,0:T(8,128)(2,1)S(1)} fusion(s32[1024]{0:T(1024)S(1)} %bitcast.179, bf16[1024,768]{1,0:T(8,128)(2,1)} %reshape.360, bf16[]{:T(256)} %constant.118.clone.1), kind=kCustom, calls=%fused_computation.62 | custom fusion | bytes 3146240 | tf_op jit(solution)/shard_map/scatter | solution.py:162
  35.1 2.7 reshape.305
  37.9 6.8 copy.136
  44.7 7.4 %all-to-all-start.1 = ((bf16[32,32,2,768]{3,2,0,1:T(2,128)(2,1)}), bf16[32,32,2,768]{3,2,0,1:T(2,128)(2,1)S(1)}, u32[]{:S(2)}, u32[]{:S(2)}) async-start(bf16[32,32,2,768]{3,2,0,1:T(2,128)(2,1)} %copy.136), calls=%async_computation.1 | async-start | bytes 6291456 | tf_op jit(solution)/shard_map/all_to_all | solution.py:166
  60.2 31.6 %all-to-all-done.1 = bf16[32,32,2,768]{3,2,0,1:T(2,128)(2,1)S(1)} async-done(((bf16[32,32,2,768]{3,2,0,1:T(2,128)(2,1)}), bf16[32,32,2,768]{3,2,0,1:T(2,128)(2,1)S(1)}, u32[]{:S(2)}, u32[]{:S(2)}) %all-to-all-start.1) | async-done | bytes 3145760 | tf_op jit(solution)/shard_map/all_to_all | solution.py:166
  94.2 7.3 %copy.138 = bf16[4,8,64,768]{2,3,1,0:T(8,128)(2,1)} copy(bf16[4,8,64,768]{3,1,0,2:T(8,128)(2,1)} %bitcast.169) | data formatting | bytes 6291456 | tf_op jit(solution)/shard_map/while | solution.py:84
  102.7 129.6 %while.27 = (s32[]{:T(128)}, f32[4,8,64,1024]{3,2,1,0:T(8,128)}, f32[4,8,64]{2,1,0:T(8,128)}, f32[4,8,64]{2,1,0:T(8,128)}, bf16[4,8,64,768]{2,3,1,0:T(8,128)(2,1...) while((s32[]{:T(128)}, f32[4,8,64,1024]{3,2,1,0:T(8,128)}, ...), condition=%wide.region_8.9_spmd, body=%wide.region_5.8_spmd.sunk | while | flops 1701051392 | bytes 57241216 | solution.py:84
  102.7 4.1 convert_bitcast_fusion.2
  112.8 9.4 %bitcast_compare_fusion.4 = pred[8,1536,1024]{2,1,0:T(32,128)(4,1)} fusion(s32[1536]{0:T(1024)S(1)} %eq.177, s32[8,96,1024]{2,1,0:T(8,128)S(1)} %dynamic-slice_bitcast_fusion.14), kind=kLoop, calls=%fused_computation.9.clone.1 | loop fusion | flops 12582912 | bytes 15734784 | tf_op jit(solution)/shard_map/while/body/eval_jaxpr/eq | solution.py:54
  122.1 11.7 %bitcast_dynamic-update-slice_fusion.5 = (f32[4,8,64,1024]{3,2,1,0:T(8,128)}, f32[8,64,1024]{2,1,0:T(8,128)S(1)}) fusion(f32[4,8,64,1024]{3,2,1,0:T(8,128)} %get-tuple-element.387, s32[]{:T(128)} %get-tuple-element.386, bf16[8,64,1536]{1,2,0:T(8,128)(2,1)S(1)} %bitcast.165, pred[8,1536,1024]{2,1,0:T(32,128)(4,1)} %bitcast_compare_fusion.4), kind=kOutput, calls=%fused_computation.12.clone.1 | convolution fusion | flops 1610612736 | bytes 18350592 | tf_op jit(solution)/shard_map/while/body/eval_jaxpr/grk,gkl->grl/dot_general | solution.py:79
  135.1 4.1 convert_bitcast_fusion.2
  145.2 9.4 %bitcast_compare_fusion.4 = pred[8,1536,1024]{2,1,0:T(32,128)(4,1)} fusion(s32[1536]{0:T(1024)S(1)} %eq.177, s32[8,96,1024]{2,1,0:T(8,128)S(1)} %dynamic-slice_bitcast_fusion.14), kind=kLoop, calls=%fused_computation.9.clone.1 | loop fusion | flops 12582912 | bytes 15734784 | tf_op jit(solution)/shard_map/while/body/eval_jaxpr/eq | solution.py:54
  154.5 11.7 %bitcast_dynamic-update-slice_fusion.5 = (f32[4,8,64,1024]{3,2,1,0:T(8,128)}, f32[8,64,1024]{2,1,0:T(8,128)S(1)}) fusion(f32[4,8,64,1024]{3,2,1,0:T(8,128)} %get-tuple-element.387, s32[]{:T(128)} %get-tuple-element.386, bf16[8,64,1536]{1,2,0:T(8,128)(2,1)S(1)} %bitcast.165, pred[8,1536,1024]{2,1,0:T(32,128)(4,1)} %bitcast_compare_fusion.4), kind=kOutput, calls=%fused_computation.12.clone.1 | convolution fusion | flops 1610612736 | bytes 18350592 | tf_op jit(solution)/shard_map/while/body/eval_jaxpr/grk,gkl->grl/dot_general | solution.py:79
  167.5 4.1 convert_bitcast_fusion.2
  177.6 9.4 %bitcast_compare_fusion.4 = pred[8,1536,1024]{2,1,0:T(32,128)(4,1)} fusion(s32[1536]{0:T(1024)S(1)} %eq.177, s32[8,96,1024]{2,1,0:T(8,128)S(1)} %dynamic-slice_bitcast_fusion.14), kind=kLoop, calls=%fused_computation.9.clone.1 | loop fusion | flops 12582912 | bytes 15734784 | tf_op jit(solution)/shard_map/while/body/eval_jaxpr/eq | solution.py:54
  186.9 11.7 %bitcast_dynamic-update-slice_fusion.5 = (f32[4,8,64,1024]{3,2,1,0:T(8,128)}, f32[8,64,1024]{2,1,0:T(8,128)S(1)}) fusion(f32[4,8,64,1024]{3,2,1,0:T(8,128)} %get-tuple-element.387, s32[]{:T(128)} %get-tuple-element.386, bf16[8,64,1536]{1,2,0:T(8,128)(2,1)S(1)} %bitcast.165, pred[8,1536,1024]{2,1,0:T(32,128)(4,1)} %bitcast_compare_fusion.4), kind=kOutput, calls=%fused_computation.12.clone.1 | convolution fusion | flops 1610612736 | bytes 18350592 | tf_op jit(solution)/shard_map/while/body/eval_jaxpr/grk,gkl->grl/dot_general | solution.py:79
  199.9 4.1 convert_bitcast_fusion.2
  210.0 9.4 %bitcast_compare_fusion.4 = pred[8,1536,1024]{2,1,0:T(32,128)(4,1)} fusion(s32[1536]{0:T(1024)S(1)} %eq.177, s32[8,96,1024]{2,1,0:T(8,128)S(1)} %dynamic-slice_bitcast_fusion.14), kind=kLoop, calls=%fused_computation.9.clone.1 | loop fusion | flops 12582912 | bytes 15734784 | tf_op jit(solution)/shard_map/while/body/eval_jaxpr/eq | solution.py:54
  219.4 11.7 %bitcast_dynamic-update-slice_fusion.5 = (f32[4,8,64,1024]{3,2,1,0:T(8,128)}, f32[8,64,1024]{2,1,0:T(8,128)S(1)}) fusion(f32[4,8,64,1024]{3,2,1,0:T(8,128)} %get-tuple-element.387, s32[]{:T(128)} %get-tuple-element.386, bf16[8,64,1536]{1,2,0:T(8,128)(2,1)S(1)} %bitcast.165, pred[8,1536,1024]{2,1,0:T(32,128)(4,1)} %bitcast_compare_fusion.4), kind=kOutput, calls=%fused_computation.12.clone.1 | convolution fusion | flops 1610612736 | bytes 18350592 | tf_op jit(solution)/shard_map/while/body/eval_jaxpr/grk,gkl->grl/dot_general | solution.py:79
  235.6 11.5 %all_to_all.35 = f32[32,32,2]{0,2,1:T(2,128)S(1)} all-to-all(f32[32,32,2]{0,2,1:T(2,128)S(1)} %get-tuple-element.256), channel_id=1, replica_groups=mesh['corpus'=32,'query'=4] {'corpus'}, dimensions={1} | all-to-all | bytes 16384 | tf_op jit(solution)/shard_map/all_to_all | solution.py:188
  247.1 4.4 all-to-all-start.4
  253.0 6.2 gather_fusion
  260.2 6.2 gather_fusion.1
  266.9 4.5 scatter_custom_fusion.3
  272.8 7.5 %all-to-all-start.5 = ((f32[32,32,2]{0,2,1:T(2,128)}), f32[32,32,2]{0,2,1:T(2,128)S(1)}, u32[]{:S(2)}, u32[]{:S(2)}) async-start(f32[32,32,2]{0,2,1:T(2,128)} %copy.148), calls=%async_computation.5 | async-start | bytes 65536 | tf_op jit(solution)/shard_map/all_to_all | solution.py:217
  280.5 4.5 scatter_custom_fusion.2
  287.6 6.2 all-to-all-start.3
  295.2 5.9 all-to-all-done.3
  301.3 212.7 %while.28 = (s32[]{:T(128)}, f32[4,8,64,768]{3,1,0,2:T(8,128)}, f32[4,16,96,8]{1,3,2,0:T(8,128)}, s32[4,8,64,9]{2,1,3,0:T(8,128)S(1)}, f32[4,8,64,1024]{3,2,1,0:...) while((s32[]{:T(128)}, f32[4,8,64,768]{3,1,0,2:T(8,128)}, ...), condition=%wide.region_15.16_spmd.clone, body=%wide.region_13.15_spmd.clone.sunk | while | flops 1788871168 | bytes 67385192 | solution.py:129
  302.3 7.1 %select_reduce_fusion.2 = f32[8,64,1024]{2,1,0:T(8,128)} fusion(f32[8]{0:T(128)S(1)} %subtract_multiply_fusion.2, s32[8,64,8]{2,1,0:T(8,128)S(1)} %copy.183), kind=kLoop, calls=%fused_computation.21.clone.1 | loop fusion | flops 12058624 | bytes 2113568 | tf_op jit(solution)/shard_map/while/body/eval_jaxpr/reduce_sum | solution.py:112
  313.6 9.3 %bitcast_compare_fusion.5 = pred[8,1536,1024]{2,1,0:T(32,128)(4,1)} fusion(s32[1536]{0:T(1024)S(1)} %eq.184, s32[8,96,1024]{2,1,0:T(8,128)S(1)} %dynamic-slice_bitcast_fusion.15), kind=kLoop, calls=%fused_computation.19.clone.1 | loop fusion | flops 12582912 | bytes 15734784 | tf_op jit(solution)/shard_map/while/body/eval_jaxpr/eq | solution.py:54
  322.9 12.8 %fusion.84 = f32[8,64,1536]{1,2,0:T(8,128)} fusion(pred[8,1536,1024]{2,1,0:T(32,128)(4,1)} %bitcast_compare_fusion.5, f32[8,64,1024]{2,1,0:T(8,128)} %select_reduce_fusion.2, f32[4,8,64,1024]{3,2,1,0:T(8,128)} %get-tuple-element.430, s32[]{:T(128)} %get-tuple-element.415, f32[8,64]{1,0:T(8,128)S(1)} %get-tuple-element.375, ...), kind=kOutput, calls=%fused_computation.38.clone.1 | convolution fusion | flops 1613234176 | bytes 19928576 | tf_op jit(solution)/shard_map/while/body/eval_jaxpr/grl,gkl->grk/dot_general | solution.py:118
  335.8 5.5 fusion.85
  343.6 2.7 constant_dynamic-update-slice_fusion.2
  346.3 8.3 %fusion.86 = f32[4,16,96,8]{1,3,2,0:T(8,128)} fusion(f32[4,16,96,8]{1,3,2,0:T(8,128)} %get-tuple-element.417, s32[]{:T(128)} %get-tuple-element.415, f32[8,64,96,16]{1,3,2,0:T(8,128)} %bitcast.164, bf16[4,8,64,768]{2,3,1,0:T(8,128)(2,1)} %get-tuple-element.435), kind=kOutput, calls=%fused_computation.37.clone.1 | convolution fusion | flops 75497472 | bytes 8258560 | tf_op jit(solution)/shard_map/while/body/eval_jaxpr/grmk,grme->kme/dot_general | solution.py:126
  355.4 7.1 %select_reduce_fusion.2 = f32[8,64,1024]{2,1,0:T(8,128)} fusion(f32[8]{0:T(128)S(1)} %subtract_multiply_fusion.2, s32[8,64,8]{2,1,0:T(8,128)S(1)} %copy.183), kind=kLoop, calls=%fused_computation.21.clone.1 | loop fusion | flops 12058624 | bytes 2113568 | tf_op jit(solution)/shard_map/while/body/eval_jaxpr/reduce_sum | solution.py:112
  366.7 9.3 %bitcast_compare_fusion.5 = pred[8,1536,1024]{2,1,0:T(32,128)(4,1)} fusion(s32[1536]{0:T(1024)S(1)} %eq.184, s32[8,96,1024]{2,1,0:T(8,128)S(1)} %dynamic-slice_bitcast_fusion.15), kind=kLoop, calls=%fused_computation.19.clone.1 | loop fusion | flops 12582912 | bytes 15734784 | tf_op jit(solution)/shard_map/while/body/eval_jaxpr/eq | solution.py:54
  376.0 12.8 %fusion.84 = f32[8,64,1536]{1,2,0:T(8,128)} fusion(pred[8,1536,1024]{2,1,0:T(32,128)(4,1)} %bitcast_compare_fusion.5, f32[8,64,1024]{2,1,0:T(8,128)} %select_reduce_fusion.2, f32[4,8,64,1024]{3,2,1,0:T(8,128)} %get-tuple-element.430, s32[]{:T(128)} %get-tuple-element.415, f32[8,64]{1,0:T(8,128)S(1)} %get-tuple-element.375, ...), kind=kOutput, calls=%fused_computation.38.clone.1 | convolution fusion | flops 1613234176 | bytes 19928576 | tf_op jit(solution)/shard_map/while/body/eval_jaxpr/grl,gkl->grk/dot_general | solution.py:118
  388.9 5.5 fusion.85
  396.7 2.7 constant_dynamic-update-slice_fusion.2
  399.4 8.2 %fusion.86 = f32[4,16,96,8]{1,3,2,0:T(8,128)} fusion(f32[4,16,96,8]{1,3,2,0:T(8,128)} %get-tuple-element.417, s32[]{:T(128)} %get-tuple-element.415, f32[8,64,96,16]{1,3,2,0:T(8,128)} %bitcast.164, bf16[4,8,64,768]{2,3,1,0:T(8,128)(2,1)} %get-tuple-element.435), kind=kOutput, calls=%fused_computation.37.clone.1 | convolution fusion | flops 75497472 | bytes 8258560 | tf_op jit(solution)/shard_map/while/body/eval_jaxpr/grmk,grme->kme/dot_general | solution.py:126
  408.4 7.1 %select_reduce_fusion.2 = f32[8,64,1024]{2,1,0:T(8,128)} fusion(f32[8]{0:T(128)S(1)} %subtract_multiply_fusion.2, s32[8,64,8]{2,1,0:T(8,128)S(1)} %copy.183), kind=kLoop, calls=%fused_computation.21.clone.1 | loop fusion | flops 12058624 | bytes 2113568 | tf_op jit(solution)/shard_map/while/body/eval_jaxpr/reduce_sum | solution.py:112
  419.8 9.3 %bitcast_compare_fusion.5 = pred[8,1536,1024]{2,1,0:T(32,128)(4,1)} fusion(s32[1536]{0:T(1024)S(1)} %eq.184, s32[8,96,1024]{2,1,0:T(8,128)S(1)} %dynamic-slice_bitcast_fusion.15), kind=kLoop, calls=%fused_computation.19.clone.1 | loop fusion | flops 12582912 | bytes 15734784 | tf_op jit(solution)/shard_map/while/body/eval_jaxpr/eq | solution.py:54
  429.1 12.8 %fusion.84 = f32[8,64,1536]{1,2,0:T(8,128)} fusion(pred[8,1536,1024]{2,1,0:T(32,128)(4,1)} %bitcast_compare_fusion.5, f32[8,64,1024]{2,1,0:T(8,128)} %select_reduce_fusion.2, f32[4,8,64,1024]{3,2,1,0:T(8,128)} %get-tuple-element.430, s32[]{:T(128)} %get-tuple-element.415, f32[8,64]{1,0:T(8,128)S(1)} %get-tuple-element.375, ...), kind=kOutput, calls=%fused_computation.38.clone.1 | convolution fusion | flops 1613234176 | bytes 19928576 | tf_op jit(solution)/shard_map/while/body/eval_jaxpr/grl,gkl->grk/dot_general | solution.py:118
  441.9 5.5 fusion.85
  449.8 2.7 constant_dynamic-update-slice_fusion.2
  452.5 8.2 %fusion.86 = f32[4,16,96,8]{1,3,2,0:T(8,128)} fusion(f32[4,16,96,8]{1,3,2,0:T(8,128)} %get-tuple-element.417, s32[]{:T(128)} %get-tuple-element.415, f32[8,64,96,16]{1,3,2,0:T(8,128)} %bitcast.164, bf16[4,8,64,768]{2,3,1,0:T(8,128)(2,1)} %get-tuple-element.435), kind=kOutput, calls=%fused_computation.37.clone.1 | convolution fusion | flops 75497472 | bytes 8258560 | tf_op jit(solution)/shard_map/while/body/eval_jaxpr/grmk,grme->kme/dot_general | solution.py:126
  461.5 7.1 %select_reduce_fusion.2 = f32[8,64,1024]{2,1,0:T(8,128)} fusion(f32[8]{0:T(128)S(1)} %subtract_multiply_fusion.2, s32[8,64,8]{2,1,0:T(8,128)S(1)} %copy.183), kind=kLoop, calls=%fused_computation.21.clone.1 | loop fusion | flops 12058624 | bytes 2113568 | tf_op jit(solution)/shard_map/while/body/eval_jaxpr/reduce_sum | solution.py:112
  472.8 9.3 %bitcast_compare_fusion.5 = pred[8,1536,1024]{2,1,0:T(32,128)(4,1)} fusion(s32[1536]{0:T(1024)S(1)} %eq.184, s32[8,96,1024]{2,1,0:T(8,128)S(1)} %dynamic-slice_bitcast_fusion.15), kind=kLoop, calls=%fused_computation.19.clone.1 | loop fusion | flops 12582912 | bytes 15734784 | tf_op jit(solution)/shard_map/while/body/eval_jaxpr/eq | solution.py:54
  482.2 12.8 %fusion.84 = f32[8,64,1536]{1,2,0:T(8,128)} fusion(pred[8,1536,1024]{2,1,0:T(32,128)(4,1)} %bitcast_compare_fusion.5, f32[8,64,1024]{2,1,0:T(8,128)} %select_reduce_fusion.2, f32[4,8,64,1024]{3,2,1,0:T(8,128)} %get-tuple-element.430, s32[]{:T(128)} %get-tuple-element.415, f32[8,64]{1,0:T(8,128)S(1)} %get-tuple-element.375, ...), kind=kOutput, calls=%fused_computation.38.clone.1 | convolution fusion | flops 1613234176 | bytes 19928576 | tf_op jit(solution)/shard_map/while/body/eval_jaxpr/grl,gkl->grk/dot_general | solution.py:118
  495.0 5.5 fusion.85
  502.8 2.7 constant_dynamic-update-slice_fusion.2
  505.6 8.2 %fusion.86 = f32[4,16,96,8]{1,3,2,0:T(8,128)} fusion(f32[4,16,96,8]{1,3,2,0:T(8,128)} %get-tuple-element.417, s32[]{:T(128)} %get-tuple-element.415, f32[8,64,96,16]{1,3,2,0:T(8,128)} %bitcast.164, bf16[4,8,64,768]{2,3,1,0:T(8,128)(2,1)} %get-tuple-element.435), kind=kOutput, calls=%fused_computation.37.clone.1 | convolution fusion | flops 75497472 | bytes 8258560 | tf_op jit(solution)/shard_map/while/body/eval_jaxpr/grmk,grme->kme/dot_general | solution.py:126
  514.1 5.0 all-to-all-start.6
  519.2 141.8 %psum.7 = f32[16,768]{0,1:T(8,128)S(1)} all-reduce(f32[16,768]{0,1:T(8,128)S(1)} %bitcast.174), channel_id=1, replica_groups=mesh['corpus'=32,'query'=4] {'corpus','query'}, use_global_device_ids=true, to_apply=%region_18.19 | all-reduce | flops 12288 | bytes 98304 | tf_op jit(solution)/shard_map/psum | solution.py:241
  663.2 10.3 %copy.154 = f32[32,32,2,768]{3,2,1,0:T(2,128)} copy(f32[32,32,2,768]{3,0,2,1:T(8,128)} %all-to-all-done.6) | data formatting | bytes 12582912 | tf_op jit(solution)/shard_map/all_to_all | solution.py:232
  673.5 8.5 %reshape.321 = f32[2048,768]{1,0:T(8,128)} reshape(f32[32,32,2,768]{3,2,1,0:T(2,128)} %copy.154) | data formatting | bytes 12582912 | tf_op jit(solution)/shard_map/reshape | solution.py:239
  682.1 8.7 %gather_fusion.2 = f32[1024,768]{1,0:T(8,128)} fusion(f32[2048,768]{1,0:T(8,128)} %reshape.321, s32[1024]{0:T(1024)S(1)} %copy-done.14), kind=kCustom, calls=%fused_computation.2 | custom fusion | bytes 6295552 | tf_op jit(solution)/shard_map/gather | solution.py:239
  690.8 3.1 reshape.322
  693.9 2.9 reduce_sum.65
  (225 shorter events, 92.1 us)
Async XLA Ops:
  2.4 1.9 copy-start.1
  9.5 0.8 copy-start.16
  10.2 16.1 %copy-start.7 = (bf16[256,768]{1,0:T(8,128)(2,1)S(1)}, bf16[256,768]{1,0:T(8,128)(2,1)}, u32[]{:S(2)}) copy-start(bf16[256,768]{1,0:T(8,128)(2,1)} %param.9) | copy-start | bytes 1179652
  10.9 17.1 %copy-start.15 = (s32[1024,1]{0,1:T(1,128)}, s32[1024,1]{0,1:T(1,128)S(1)}, u32[]{:S(2)}) copy-start(s32[1024,1]{0,1:T(1,128)S(1)} %compare_select_fusion.1) | copy-start | bytes 12292
  16.7 28.0 %all-to-all-start = ((s32[32,1,576]{2,1,0:T(1,128)}), s32[32,1,576]{2,1,0:T(1,128)S(1)}, u32[]{:S(2)}, u32[]{:S(2)}) async-start(s32[32,1,576]{2,1,0:T(1,128)} %reshape.393), calls=%async_computation | async-start | bytes 163840 | tf_op jit(solution)/shard_map/all_to_all | solution.py:173
  44.7 7.4 %copy-start.8 = (s32[32,1,576]{2,1,0:T(1,128)}, s32[32,1,576]{2,1,0:T(1,128)S(1)}, u32[]{:S(2)}) copy-start(s32[32,1,576]{2,1,0:T(1,128)S(1)} %all-to-all-done) | copy-start | bytes 221188
  44.7 47.1 %all-to-all-start.1 = ((bf16[32,32,2,768]{3,2,0,1:T(2,128)(2,1)}), bf16[32,32,2,768]{3,2,0,1:T(2,128)(2,1)S(1)}, u32[]{:S(2)}, u32[]{:S(2)}) async-start(bf16[32,32,2,768]{3,2,0,1:T(2,128)(2,1)} %copy.136), calls=%async_computation.1 | async-start | bytes 6291456 | tf_op jit(solution)/shard_map/all_to_all | solution.py:166
  58.8 0.7 copy-start.3
  112.8 9.4 %copy-start = (bf16[8,64,96,16]{1,3,2,0:T(8,128)(2,1)S(1)}, bf16[8,64,96,16]{1,3,2,0:T(8,128)(2,1)}, u32[]{:S(2)}) copy-start(bf16[8,64,96,16]{1,3,2,0:T(8,128)(2,1)} %copy.181) | copy-start | bytes 4718596 | tf_op jit(solution)/shard_map/while
  145.2 9.4 %copy-start = (bf16[8,64,96,16]{1,3,2,0:T(8,128)(2,1)S(1)}, bf16[8,64,96,16]{1,3,2,0:T(8,128)(2,1)}, u32[]{:S(2)}) copy-start(bf16[8,64,96,16]{1,3,2,0:T(8,128)(2,1)} %copy.181) | copy-start | bytes 4718596 | tf_op jit(solution)/shard_map/while
  177.6 9.4 %copy-start = (bf16[8,64,96,16]{1,3,2,0:T(8,128)(2,1)S(1)}, bf16[8,64,96,16]{1,3,2,0:T(8,128)(2,1)}, u32[]{:S(2)}) copy-start(bf16[8,64,96,16]{1,3,2,0:T(8,128)(2,1)} %copy.181) | copy-start | bytes 4718596 | tf_op jit(solution)/shard_map/while
  210.0 9.4 %copy-start = (bf16[8,64,96,16]{1,3,2,0:T(8,128)(2,1)S(1)}, bf16[8,64,96,16]{1,3,2,0:T(8,128)(2,1)}, u32[]{:S(2)}) copy-start(bf16[8,64,96,16]{1,3,2,0:T(8,128)(2,1)} %copy.181) | copy-start | bytes 4718596 | tf_op jit(solution)/shard_map/while
  247.1 12.3 %all-to-all-start.4 = ((f32[32,32,2]{0,2,1:T(2,128)}), f32[32,32,2]{0,2,1:T(2,128)S(1)}, u32[]{:S(2)}, u32[]{:S(2)}) async-start(f32[32,32,2]{0,2,1:T(2,128)} %get-tuple-element.255), calls=%async_computation.4 | async-start | bytes 65536 | tf_op jit(solution)/shard_map/all_to_all | solution.py:195
  252.2 14.2 %copy-start.13 = (s32[1024]{0:T(1024)}, s32[1024]{0:T(1024)S(1)}, u32[]{:S(2)}) copy-start(s32[1024]{0:T(1024)S(1)} %broadcast_clamp_fusion) | copy-start | bytes 12292
  259.4 34.5 %copy-start.4 = (s32[32,32,2,9]{0,2,1,3:T(2,128)S(1)}, s32[32,32,2,9]{0,2,1,3:T(2,128)}, u32[]{:S(2)}) copy-start(s32[32,32,2,9]{0,2,1,3:T(2,128)} %copy-done.3) | copy-start | bytes 221188
  272.8 14.8 %all-to-all-start.5 = ((f32[32,32,2]{0,2,1:T(2,128)}), f32[32,32,2]{0,2,1:T(2,128)S(1)}, u32[]{:S(2)}, u32[]{:S(2)}) async-start(f32[32,32,2]{0,2,1:T(2,128)} %copy.148), calls=%async_computation.5 | async-start | bytes 65536 | tf_op jit(solution)/shard_map/all_to_all | solution.py:217
  287.6 13.5 %all-to-all-start.3 = ((f32[32,32,2]{0,2,1:T(2,128)}), f32[32,32,2]{0,2,1:T(2,128)S(1)}, u32[]{:S(2)}, u32[]{:S(2)}) async-start(f32[32,32,2]{0,2,1:T(2,128)} %copy.144), calls=%async_computation.3 | async-start | bytes 65536 | tf_op jit(solution)/shard_map/all_to_all | solution.py:210
  301.5 0.6 copy-start.9
  301.5 0.6 copy-start.11
  301.5 8.5 %copy-start.5 = (s32[4,8,64,9]{2,1,3,0:T(8,128)}, s32[4,8,64,9]{2,1,3,0:T(8,128)S(1)}, u32[]{:S(2)}) copy-start(s32[4,8,64,9]{2,1,3,0:T(8,128)S(1)} %get-tuple-element.429) | copy-start | bytes 221188 | tf_op jit(solution)/shard_map/while
  346.3 8.3 %copy-start.6 = (s32[4,8,64,9]{2,1,3,0:T(8,128)S(1)}, s32[4,8,64,9]{2,1,3,0:T(8,128)}, u32[]{:S(2)}) copy-start(s32[4,8,64,9]{2,1,3,0:T(8,128)} %copy-done.5) | copy-start | bytes 221188 | tf_op jit(solution)/shard_map/while
  346.3 8.3 %copy-start.10 = (f32[4,8,64]{2,1,0:T(8,128)S(1)}, f32[4,8,64]{2,1,0:T(8,128)}, u32[]{:S(2)}) copy-start(f32[4,8,64]{2,1,0:T(8,128)} %copy-done.9) | copy-start | bytes 24580 | tf_op jit(solution)/shard_map/while
  346.3 8.3 %copy-start.12 = (f32[4,8,64]{2,1,0:T(8,128)S(1)}, f32[4,8,64]{2,1,0:T(8,128)}, u32[]{:S(2)}) copy-start(f32[4,8,64]{2,1,0:T(8,128)} %copy-done.11) | copy-start | bytes 24580 | tf_op jit(solution)/shard_map/while
  354.6 0.6 copy-start.9
  354.6 0.6 copy-start.11
  354.6 8.5 %copy-start.5 = (s32[4,8,64,9]{2,1,3,0:T(8,128)}, s32[4,8,64,9]{2,1,3,0:T(8,128)S(1)}, u32[]{:S(2)}) copy-start(s32[4,8,64,9]{2,1,3,0:T(8,128)S(1)} %get-tuple-element.429) | copy-start | bytes 221188 | tf_op jit(solution)/shard_map/while
  399.4 8.2 %copy-start.6 = (s32[4,8,64,9]{2,1,3,0:T(8,128)S(1)}, s32[4,8,64,9]{2,1,3,0:T(8,128)}, u32[]{:S(2)}) copy-start(s32[4,8,64,9]{2,1,3,0:T(8,128)} %copy-done.5) | copy-start | bytes 221188 | tf_op jit(solution)/shard_map/while
  399.4 8.2 %copy-start.10 = (f32[4,8,64]{2,1,0:T(8,128)S(1)}, f32[4,8,64]{2,1,0:T(8,128)}, u32[]{:S(2)}) copy-start(f32[4,8,64]{2,1,0:T(8,128)} %copy-done.9) | copy-start | bytes 24580 | tf_op jit(solution)/shard_map/while
  399.4 8.2 %copy-start.12 = (f32[4,8,64]{2,1,0:T(8,128)S(1)}, f32[4,8,64]{2,1,0:T(8,128)}, u32[]{:S(2)}) copy-start(f32[4,8,64]{2,1,0:T(8,128)} %copy-done.11) | copy-start | bytes 24580 | tf_op jit(solution)/shard_map/while
  407.7 0.6 copy-start.9
  407.7 0.6 copy-start.11
  407.7 8.5 %copy-start.5 = (s32[4,8,64,9]{2,1,3,0:T(8,128)}, s32[4,8,64,9]{2,1,3,0:T(8,128)S(1)}, u32[]{:S(2)}) copy-start(s32[4,8,64,9]{2,1,3,0:T(8,128)S(1)} %get-tuple-element.429) | copy-start | bytes 221188 | tf_op jit(solution)/shard_map/while
  452.5 8.3 %copy-start.6 = (s32[4,8,64,9]{2,1,3,0:T(8,128)S(1)}, s32[4,8,64,9]{2,1,3,0:T(8,128)}, u32[]{:S(2)}) copy-start(s32[4,8,64,9]{2,1,3,0:T(8,128)} %copy-done.5) | copy-start | bytes 221188 | tf_op jit(solution)/shard_map/while
  452.5 8.3 %copy-start.10 = (f32[4,8,64]{2,1,0:T(8,128)S(1)}, f32[4,8,64]{2,1,0:T(8,128)}, u32[]{:S(2)}) copy-start(f32[4,8,64]{2,1,0:T(8,128)} %copy-done.9) | copy-start | bytes 24580 | tf_op jit(solution)/shard_map/while
  452.5 8.3 %copy-start.12 = (f32[4,8,64]{2,1,0:T(8,128)S(1)}, f32[4,8,64]{2,1,0:T(8,128)}, u32[]{:S(2)}) copy-start(f32[4,8,64]{2,1,0:T(8,128)} %copy-done.11) | copy-start | bytes 24580 | tf_op jit(solution)/shard_map/while
  460.7 0.6 copy-start.9
  460.8 0.6 copy-start.11
  460.8 8.5 %copy-start.5 = (s32[4,8,64,9]{2,1,3,0:T(8,128)}, s32[4,8,64,9]{2,1,3,0:T(8,128)S(1)}, u32[]{:S(2)}) copy-start(s32[4,8,64,9]{2,1,3,0:T(8,128)S(1)} %get-tuple-element.429) | copy-start | bytes 221188 | tf_op jit(solution)/shard_map/while
  505.6 8.2 %copy-start.6 = (s32[4,8,64,9]{2,1,3,0:T(8,128)S(1)}, s32[4,8,64,9]{2,1,3,0:T(8,128)}, u32[]{:S(2)}) copy-start(s32[4,8,64,9]{2,1,3,0:T(8,128)} %copy-done.5) | copy-start | bytes 221188 | tf_op jit(solution)/shard_map/while
  505.6 8.2 %copy-start.10 = (f32[4,8,64]{2,1,0:T(8,128)S(1)}, f32[4,8,64]{2,1,0:T(8,128)}, u32[]{:S(2)}) copy-start(f32[4,8,64]{2,1,0:T(8,128)} %copy-done.9) | copy-start | bytes 24580 | tf_op jit(solution)/shard_map/while
  505.6 8.2 %copy-start.12 = (f32[4,8,64]{2,1,0:T(8,128)S(1)}, f32[4,8,64]{2,1,0:T(8,128)}, u32[]{:S(2)}) copy-start(f32[4,8,64]{2,1,0:T(8,128)} %copy-done.11) | copy-start | bytes 24580 | tf_op jit(solution)/shard_map/while
  514.0 5.0 copy-start.2
  514.1 149.2 %all-to-all-start.6 = ((f32[32,32,2,768]{3,0,2,1:T(8,128)}), f32[32,32,2,768]{3,0,2,1:T(8,128)}, u32[]{:S(2)}, u32[]{:S(2)}) async-start(f32[32,32,2,768]{3,0,2,1:T(8,128)} %bitcast.170), calls=%async_computation.6 | async-start | bytes 12582912 | tf_op jit(solution)/shard_map/all_to_all | solution.py:232
  673.5 8.5 %copy-start.14 = (s32[1024]{0:T(1024)S(1)}, s32[1024]{0:T(1024)}, u32[]{:S(2)}) copy-start(s32[1024]{0:T(1024)} %copy-done.13) | copy-start | bytes 12292
where the time goes:
time: 708 us; the launch traced here: 697 us
  matrix products  170 us (24%)
  local copies, waits for them, and re-layouts  168 us (24%)
  blocking collectives  153 us (22%)
  other arithmetic  125 us (18%)
  starting transfers between devices  40.1 us (6%)
  waiting for transfers between devices  38.7 us (5%)
    psum x1, blocking collectives, shards(): book_sum = lax.psum(book_part, ('corpus', 'query'))  142 us
    eq x8, other arithmetic, code_one_hot(): marked = code_block[:, :, None, :] == levels[None, None, :, None]  74.8 us
    dot_general x4, matrix products, grad_piece(): jnp.einsum('grl,gkl->grk', grad_scores, one_hot, preferred_element_type=j...  51.3 us
    dot_general x4, matrix products, score_piece(): jnp.einsum('grk,gkl->grl', lut_rows, one_hot, preferred_element_type=jnp....  46.8 us
    dot_general x4, matrix products, grad_piece(): jnp.einsum('grmk,grme->kme', histogram, split_rows, precision=highest)  33 us
    all_to_all x1, waiting for transfers between devices, shards(): lax.all_to_all(sending.reshape(lists_dev, corpus_size, capacity, D), 'cor...  31.6 us
    eq x24, local copies, waits for them, and re-layouts, code_one_hot(): marked = code_block[:, :, None, :] == levels[None, None, :, None]  28.9 us
    reduce_sum x4, other arithmetic, grad_piece(): jnp.sum(jnp.where(target_spot[:, :, :, None] == places, weights[:, None],...  28.5 us
  transfers between devices with their start and end apart: 6, of which 3 were waited for; matrix products, arithmetic and copies ran while one was open for 6% of the time, Pallas kernels for 0%

commit v1 on v0

--- a/solution.py
+++ b/solution.py
@@ -1,3 +1,4 @@
+import functools
 import jax
 import jax.numpy as jnp
 from jax import lax
@@ -12,6 +13,13 @@
 TARGETS = 8
 NEGATIVE = -1e30
 EPSILON = 1e-06
+
+
+def _extend_record(inputs, dev_axis, mesh_ax):
+    return jax.lax.psum(jax.lax.psum(inputs, dev_axis), mesh_ax)
+
+
+lift_values = functools.partial(_extend_record, dev_axis="query", mesh_ax="corpus")
 
 
 def rank_weights():
@@ -238,7 +246,7 @@
     )
     per_probe = returned.reshape(slot_count, D)[placed].reshape(query_rows, PROBES, D)
     grad_queries = jnp.sum(per_probe, axis=1)
-    book_sum = lax.psum(book_part, ("corpus", "query"))
+    book_sum = lift_values(book_part)
     normed = book_sum * lax.rsqrt(jnp.mean(book_sum * book_sum) + EPSILON)
     return (grad_queries.astype(jnp.bfloat16), normed)
 

time: 708 us -> 759 us (1.072)
  blocking collectives: 153 us -> 200 us
    psum x1 -> x2, blocking collectives: 142 us -> 189 us  [_extend_record(): return jax.lax.psum(jax.lax.psum(inputs, dev_axis), mesh_ax)]
where the time goes in v1:
time: 759 us; the launch traced here: 744 us
  blocking collectives  200 us (26%)
  matrix products  170 us (22%)
  local copies, waits for them, and re-layouts  168 us (22%)
  other arithmetic  125 us (16%)
  starting transfers between devices  40.1 us (5%)
  waiting for transfers between devices  38.7 us (5%)
    psum x2, blocking collectives, _extend_record(): return jax.lax.psum(jax.lax.psum(inputs, dev_axis), mesh_ax)  189 us
    eq x8, other arithmetic, code_one_hot(): marked = code_block[:, :, None, :] == levels[None, None, :, None]  74.8 us
    dot_general x4, matrix products, grad_piece(): jnp.einsum('grl,gkl->grk', grad_scores, one_hot, preferred_element_type=j...  51.3 us
    dot_general x4, matrix products, score_piece(): jnp.einsum('grk,gkl->grl', lut_rows, one_hot, preferred_element_type=jnp....  46.8 us
    dot_general x4, matrix products, grad_piece(): jnp.einsum('grmk,grme->kme', histogram, split_rows, precision=highest)  33 us
    all_to_all x1, waiting for transfers between devices, shards(): lax.all_to_all(sending.reshape(lists_dev, corpus_size, capacity, D), 'cor...  31.6 us
    eq x24, local copies, waits for them, and re-layouts, code_one_hot(): marked = code_block[:, :, None, :] == levels[None, None, :, None]  28.9 us
    reduce_sum x4, other arithmetic, grad_piece(): jnp.sum(jnp.where(target_spot[:, :, :, None] == places, weights[:, None],...  28.5 us
  transfers between devices with their start and end apart: 6, of which 3 were waited for; matrix products, arithmetic and copies ran while one was open for 6% of the time, Pallas kernels for 0%

profile of v1, /device:TPU:1, one launch (start us, length us, event | category | flops | bytes accessed | tf_op | source)
XLA Modules:
  0.0 743.9 jit_solution(16586258859005661835)
XLA Ops:
  4.4 2.6 broadcast_add_fusion
  11.3 3.6 scatter_custom_fusion
  16.7 9.6 %all-to-all-start = ((s32[32,1,576]{2,1,0:T(1,128)}), s32[32,1,576]{2,1,0:T(1,128)S(1)}, u32[]{:S(2)}, u32[]{:S(2)}) async-start(s32[32,1,576]{2,1,0:T(1,128)} %reshape.393), calls=%async_computation | async-start | bytes 163840 | tf_op jit(solution)/shard_map/all_to_all | solution.py:181
  28.1 7.1 scatter_custom_fusion.1
  35.1 2.7 reshape.305
  37.9 6.8 copy.136
  44.7 7.4 all-to-all-start.1
  60.2 31.6 %all-to-all-done.1 = bf16[32,32,2,768]{3,2,0,1:T(2,128)(2,1)S(1)} async-done(((bf16[32,32,2,768]{3,2,0,1:T(2,128)(2,1)}), bf16[32,32,2,768]{3,2,0,1:T(2,128)(2,1)S(1)}, u32[]{:S(2)}, u32[]{:S(2)}) %all-to-all-start.1) | async-done | bytes 3145760 | tf_op jit(solution)/shard_map/all_to_all | solution.py:174
  94.2 7.3 copy.138
  102.7 129.6 %while.27 = (s32[]{:T(128)}, f32[4,8,64,1024]{3,2,1,0:T(8,128)}, f32[4,8,64]{2,1,0:T(8,128)}, f32[4,8,64]{2,1,0:T(8,128)}, bf16[4,8,64,768]{2,3,1,0:T(8,128)(2,1...) while((s32[]{:T(128)}, f32[4,8,64,1024]{3,2,1,0:T(8,128)}, ...), condition=%wide.region_8.9_spmd, body=%wide.region_5.8_spmd.sunk | while | flops 1701051392 | bytes 57241216 | solution.py:92
  102.7 4.1 convert_bitcast_fusion.2
  112.8 9.4 %bitcast_compare_fusion.4 = pred[8,1536,1024]{2,1,0:T(32,128)(4,1)} fusion(s32[1536]{0:T(1024)S(1)} %eq.177, s32[8,96,1024]{2,1,0:T(8,128)S(1)} %dynamic-slice_bitcast_fusion.14), kind=kLoop, calls=%fused_computation.9.clone.1 | loop fusion | flops 12582912 | bytes 15734784 | tf_op jit(solution)/shard_map/while/body/eval_jaxpr/eq | solution.py:62
  122.1 11.7 %bitcast_dynamic-update-slice_fusion.5 = (f32[4,8,64,1024]{3,2,1,0:T(8,128)}, f32[8,64,1024]{2,1,0:T(8,128)S(1)}) fusion(f32[4,8,64,1024]{3,2,1,0:T(8,128)} %get-tuple-element.387, s32[]{:T(128)} %get-tuple-element.386, bf16[8,64,1536]{1,2,0:T(8,128)(2,1)S(1)} %bitcast.165, pred[8,1536,1024]{2,1,0:T(32,128)(4,1)} %bitcast_compare_fusion.4), kind=kOutput, calls=%fused_computation.12.clone.1 | convolution fusion | flops 1610612736 | bytes 18350592 | tf_op jit(solution)/shard_map/while/body/eval_jaxpr/grk,gkl->grl/dot_general | solution.py:87
  135.1 4.1 convert_bitcast_fusion.2
  145.2 9.4 %bitcast_compare_fusion.4 = pred[8,1536,1024]{2,1,0:T(32,128)(4,1)} fusion(s32[1536]{0:T(1024)S(1)} %eq.177, s32[8,96,1024]{2,1,0:T(8,128)S(1)} %dynamic-slice_bitcast_fusion.14), kind=kLoop, calls=%fused_computation.9.clone.1 | loop fusion | flops 12582912 | bytes 15734784 | tf_op jit(solution)/shard_map/while/body/eval_jaxpr/eq | solution.py:62
  154.5 11.7 %bitcast_dynamic-update-slice_fusion.5 = (f32[4,8,64,1024]{3,2,1,0:T(8,128)}, f32[8,64,1024]{2,1,0:T(8,128)S(1)}) fusion(f32[4,8,64,1024]{3,2,1,0:T(8,128)} %get-tuple-element.387, s32[]{:T(128)} %get-tuple-element.386, bf16[8,64,1536]{1,2,0:T(8,128)(2,1)S(1)} %bitcast.165, pred[8,1536,1024]{2,1,0:T(32,128)(4,1)} %bitcast_compare_fusion.4), kind=kOutput, calls=%fused_computation.12.clone.1 | convolution fusion | flops 1610612736 | bytes 18350592 | tf_op jit(solution)/shard_map/while/body/eval_jaxpr/grk,gkl->grl/dot_general | solution.py:87
  167.5 4.1 convert_bitcast_fusion.2
  177.6 9.4 %bitcast_compare_fusion.4 = pred[8,1536,1024]{2,1,0:T(32,128)(4,1)} fusion(s32[1536]{0:T(1024)S(1)} %eq.177, s32[8,96,1024]{2,1,0:T(8,128)S(1)} %dynamic-slice_bitcast_fusion.14), kind=kLoop, calls=%fused_computation.9.clone.1 | loop fusion | flops 12582912 | bytes 15734784 | tf_op jit(solution)/shard_map/while/body/eval_jaxpr/eq | solution.py:62
  186.9 11.7 %bitcast_dynamic-update-slice_fusion.5 = (f32[4,8,64,1024]{3,2,1,0:T(8,128)}, f32[8,64,1024]{2,1,0:T(8,128)S(1)}) fusion(f32[4,8,64,1024]{3,2,1,0:T(8,128)} %get-tuple-element.387, s32[]{:T(128)} %get-tuple-element.386, bf16[8,64,1536]{1,2,0:T(8,128)(2,1)S(1)} %bitcast.165, pred[8,1536,1024]{2,1,0:T(32,128)(4,1)} %bitcast_compare_fusion.4), kind=kOutput, calls=%fused_computation.12.clone.1 | convolution fusion | flops 1610612736 | bytes 18350592 | tf_op jit(solution)/shard_map/while/body/eval_jaxpr/grk,gkl->grl/dot_general | solution.py:87
  199.9 4.1 convert_bitcast_fusion.2
  210.0 9.4 %bitcast_compare_fusion.4 = pred[8,1536,1024]{2,1,0:T(32,128)(4,1)} fusion(s32[1536]{0:T(1024)S(1)} %eq.177, s32[8,96,1024]{2,1,0:T(8,128)S(1)} %dynamic-slice_bitcast_fusion.14), kind=kLoop, calls=%fused_computation.9.clone.1 | loop fusion | flops 12582912 | bytes 15734784 | tf_op jit(solution)/shard_map/while/body/eval_jaxpr/eq | solution.py:62
  219.4 11.7 %bitcast_dynamic-update-slice_fusion.5 = (f32[4,8,64,1024]{3,2,1,0:T(8,128)}, f32[8,64,1024]{2,1,0:T(8,128)S(1)}) fusion(f32[4,8,64,1024]{3,2,1,0:T(8,128)} %get-tuple-element.387, s32[]{:T(128)} %get-tuple-element.386, bf16[8,64,1536]{1,2,0:T(8,128)(2,1)S(1)} %bitcast.165, pred[8,1536,1024]{2,1,0:T(32,128)(4,1)} %bitcast_compare_fusion.4), kind=kOutput, calls=%fused_computation.12.clone.1 | convolution fusion | flops 1610612736 | bytes 18350592 | tf_op jit(solution)/shard_map/while/body/eval_jaxpr/grk,gkl->grl/dot_general | solution.py:87
  235.6 11.5 %all_to_all.35 = f32[32,32,2]{0,2,1:T(2,128)S(1)} all-to-all(f32[32,32,2]{0,2,1:T(2,128)S(1)} %get-tuple-element.256), channel_id=1, replica_groups=mesh['corpus'=32,'query'=4] {'corpus'}, dimensions={1} | all-to-all | bytes 16384 | tf_op jit(solution)/shard_map/all_to_all | solution.py:196
  247.1 4.4 all-to-all-start.4
  253.0 6.2 gather_fusion
  260.2 6.2 gather_fusion.1
  266.9 4.5 scatter_custom_fusion.3
  272.8 7.5 %all-to-all-start.5 = ((f32[32,32,2]{0,2,1:T(2,128)}), f32[32,32,2]{0,2,1:T(2,128)S(1)}, u32[]{:S(2)}, u32[]{:S(2)}) async-start(f32[32,32,2]{0,2,1:T(2,128)} %copy.148), calls=%async_computation.5 | async-start | bytes 65536 | tf_op jit(solution)/shard_map/all_to_all | solution.py:225
  280.5 4.5 scatter_custom_fusion.2
  287.6 6.2 all-to-all-start.3
  295.2 5.9 all-to-all-done.3
  301.3 212.7 %while.28 = (s32[]{:T(128)}, f32[4,8,64,768]{3,1,0,2:T(8,128)}, f32[4,16,96,8]{1,3,2,0:T(8,128)}, s32[4,8,64,9]{2,1,3,0:T(8,128)S(1)}, f32[4,8,64,1024]{3,2,1,0:...) while((s32[]{:T(128)}, f32[4,8,64,768]{3,1,0,2:T(8,128)}, ...), condition=%wide.region_15.16_spmd.clone, body=%wide.region_13.15_spmd.clone.sunk | while | flops 1788871168 | bytes 67385192 | solution.py:137
  302.3 7.1 select_reduce_fusion.2
  313.6 9.3 %bitcast_compare_fusion.5 = pred[8,1536,1024]{2,1,0:T(32,128)(4,1)} fusion(s32[1536]{0:T(1024)S(1)} %eq.184, s32[8,96,1024]{2,1,0:T(8,128)S(1)} %dynamic-slice_bitcast_fusion.15), kind=kLoop, calls=%fused_computation.19.clone.1 | loop fusion | flops 12582912 | bytes 15734784 | tf_op jit(solution)/shard_map/while/body/eval_jaxpr/eq | solution.py:62
  322.9 12.8 %fusion.84 = f32[8,64,1536]{1,2,0:T(8,128)} fusion(pred[8,1536,1024]{2,1,0:T(32,128)(4,1)} %bitcast_compare_fusion.5, f32[8,64,1024]{2,1,0:T(8,128)} %select_reduce_fusion.2, f32[4,8,64,1024]{3,2,1,0:T(8,128)} %get-tuple-element.430, s32[]{:T(128)} %get-tuple-element.415, f32[8,64]{1,0:T(8,128)S(1)} %get-tuple-element.375, ...), kind=kOutput, calls=%fused_computation.38.clone.1 | convolution fusion | flops 1613234176 | bytes 19928576 | tf_op jit(solution)/shard_map/while/body/eval_jaxpr/grl,gkl->grk/dot_general | solution.py:126
  335.8 5.5 fusion.85
  343.6 2.7 constant_dynamic-update-slice_fusion.2
  346.3 8.3 %fusion.86 = f32[4,16,96,8]{1,3,2,0:T(8,128)} fusion(f32[4,16,96,8]{1,3,2,0:T(8,128)} %get-tuple-element.417, s32[]{:T(128)} %get-tuple-element.415, f32[8,64,96,16]{1,3,2,0:T(8,128)} %bitcast.164, bf16[4,8,64,768]{2,3,1,0:T(8,128)(2,1)} %get-tuple-element.435), kind=kOutput, calls=%fused_computation.37.clone.1 | convolution fusion | flops 75497472 | bytes 8258560 | tf_op jit(solution)/shard_map/while/body/eval_jaxpr/grmk,grme->kme/dot_general | solution.py:134
  355.4 7.1 select_reduce_fusion.2
  366.7 9.3 %bitcast_compare_fusion.5 = pred[8,1536,1024]{2,1,0:T(32,128)(4,1)} fusion(s32[1536]{0:T(1024)S(1)} %eq.184, s32[8,96,1024]{2,1,0:T(8,128)S(1)} %dynamic-slice_bitcast_fusion.15), kind=kLoop, calls=%fused_computation.19.clone.1 | loop fusion | flops 12582912 | bytes 15734784 | tf_op jit(solution)/shard_map/while/body/eval_jaxpr/eq | solution.py:62
  376.0 12.8 %fusion.84 = f32[8,64,1536]{1,2,0:T(8,128)} fusion(pred[8,1536,1024]{2,1,0:T(32,128)(4,1)} %bitcast_compare_fusion.5, f32[8,64,1024]{2,1,0:T(8,128)} %select_reduce_fusion.2, f32[4,8,64,1024]{3,2,1,0:T(8,128)} %get-tuple-element.430, s32[]{:T(128)} %get-tuple-element.415, f32[8,64]{1,0:T(8,128)S(1)} %get-tuple-element.375, ...), kind=kOutput, calls=%fused_computation.38.clone.1 | convolution fusion | flops 1613234176 | bytes 19928576 | tf_op jit(solution)/shard_map/while/body/eval_jaxpr/grl,gkl->grk/dot_general | solution.py:126
  388.9 5.5 fusion.85
  396.7 2.7 constant_dynamic-update-slice_fusion.2
  399.4 8.2 %fusion.86 = f32[4,16,96,8]{1,3,2,0:T(8,128)} fusion(f32[4,16,96,8]{1,3,2,0:T(8,128)} %get-tuple-element.417, s32[]{:T(128)} %get-tuple-element.415, f32[8,64,96,16]{1,3,2,0:T(8,128)} %bitcast.164, bf16[4,8,64,768]{2,3,1,0:T(8,128)(2,1)} %get-tuple-element.435), kind=kOutput, calls=%fused_computation.37.clone.1 | convolution fusion | flops 75497472 | bytes 8258560 | tf_op jit(solution)/shard_map/while/body/eval_jaxpr/grmk,grme->kme/dot_general | solution.py:134
  408.4 7.1 select_reduce_fusion.2
  419.8 9.3 %bitcast_compare_fusion.5 = pred[8,1536,1024]{2,1,0:T(32,128)(4,1)} fusion(s32[1536]{0:T(1024)S(1)} %eq.184, s32[8,96,1024]{2,1,0:T(8,128)S(1)} %dynamic-slice_bitcast_fusion.15), kind=kLoop, calls=%fused_computation.19.clone.1 | loop fusion | flops 12582912 | bytes 15734784 | tf_op jit(solution)/shard_map/while/body/eval_jaxpr/eq | solution.py:62
  429.1 12.8 %fusion.84 = f32[8,64,1536]{1,2,0:T(8,128)} fusion(pred[8,1536,1024]{2,1,0:T(32,128)(4,1)} %bitcast_compare_fusion.5, f32[8,64,1024]{2,1,0:T(8,128)} %select_reduce_fusion.2, f32[4,8,64,1024]{3,2,1,0:T(8,128)} %get-tuple-element.430, s32[]{:T(128)} %get-tuple-element.415, f32[8,64]{1,0:T(8,128)S(1)} %get-tuple-element.375, ...), kind=kOutput, calls=%fused_computation.38.clone.1 | convolution fusion | flops 1613234176 | bytes 19928576 | tf_op jit(solution)/shard_map/while/body/eval_jaxpr/grl,gkl->grk/dot_general | solution.py:126
  441.9 5.5 fusion.85
  449.8 2.7 constant_dynamic-update-slice_fusion.2
  452.5 8.2 %fusion.86 = f32[4,16,96,8]{1,3,2,0:T(8,128)} fusion(f32[4,16,96,8]{1,3,2,0:T(8,128)} %get-tuple-element.417, s32[]{:T(128)} %get-tuple-element.415, f32[8,64,96,16]{1,3,2,0:T(8,128)} %bitcast.164, bf16[4,8,64,768]{2,3,1,0:T(8,128)(2,1)} %get-tuple-element.435), kind=kOutput, calls=%fused_computation.37.clone.1 | convolution fusion | flops 75497472 | bytes 8258560 | tf_op jit(solution)/shard_map/while/body/eval_jaxpr/grmk,grme->kme/dot_general | solution.py:134
  461.5 7.1 select_reduce_fusion.2
  472.8 9.3 %bitcast_compare_fusion.5 = pred[8,1536,1024]{2,1,0:T(32,128)(4,1)} fusion(s32[1536]{0:T(1024)S(1)} %eq.184, s32[8,96,1024]{2,1,0:T(8,128)S(1)} %dynamic-slice_bitcast_fusion.15), kind=kLoop, calls=%fused_computation.19.clone.1 | loop fusion | flops 12582912 | bytes 15734784 | tf_op jit(solution)/shard_map/while/body/eval_jaxpr/eq | solution.py:62
  482.2 12.8 %fusion.84 = f32[8,64,1536]{1,2,0:T(8,128)} fusion(pred[8,1536,1024]{2,1,0:T(32,128)(4,1)} %bitcast_compare_fusion.5, f32[8,64,1024]{2,1,0:T(8,128)} %select_reduce_fusion.2, f32[4,8,64,1024]{3,2,1,0:T(8,128)} %get-tuple-element.430, s32[]{:T(128)} %get-tuple-element.415, f32[8,64]{1,0:T(8,128)S(1)} %get-tuple-element.375, ...), kind=kOutput, calls=%fused_computation.38.clone.1 | convolution fusion | flops 1613234176 | bytes 19928576 | tf_op jit(solution)/shard_map/while/body/eval_jaxpr/grl,gkl->grk/dot_general | solution.py:126
  495.0 5.5 fusion.85
  502.8 2.7 constant_dynamic-update-slice_fusion.2
  505.6 8.2 %fusion.86 = f32[4,16,96,8]{1,3,2,0:T(8,128)} fusion(f32[4,16,96,8]{1,3,2,0:T(8,128)} %get-tuple-element.417, s32[]{:T(128)} %get-tuple-element.415, f32[8,64,96,16]{1,3,2,0:T(8,128)} %bitcast.164, bf16[4,8,64,768]{2,3,1,0:T(8,128)(2,1)} %get-tuple-element.435), kind=kOutput, calls=%fused_computation.37.clone.1 | convolution fusion | flops 75497472 | bytes 8258560 | tf_op jit(solution)/shard_map/while/body/eval_jaxpr/grmk,grme->kme/dot_general | solution.py:134
  514.1 5.0 all-to-all-start.6
  519.2 18.1 %psum.14 = f32[16,768]{0,1:T(8,128)S(1)} all-reduce(f32[16,768]{0,1:T(8,128)S(1)} %bitcast.174), channel_id=1, replica_groups=mesh['corpus'=32,'query'=4] {'query'}, use_global_device_ids=true, to_apply=%region_18.19 | all-reduce | flops 12288 | bytes 98304 | tf_op jit(solution)/shard_map/psum | solution.py:19
  537.3 170.5 %psum.15 = f32[16,768]{0,1:T(8,128)S(1)} all-reduce(f32[16,768]{0,1:T(8,128)S(1)} %psum.14), channel_id=1, replica_groups=mesh['corpus'=32,'query'=4] {'corpus'}, use_global_device_ids=true, to_apply=%region_19.20 | all-reduce | flops 12288 | bytes 98304 | tf_op jit(solution)/shard_map/psum | solution.py:19
  710.0 10.3 %copy.154 = f32[32,32,2,768]{3,2,1,0:T(2,128)} copy(f32[32,32,2,768]{3,0,2,1:T(8,128)} %all-to-all-done.6) | data formatting | bytes 12582912 | tf_op jit(solution)/shard_map/all_to_all | solution.py:240
  720.3 8.5 %reshape.321 = f32[2048,768]{1,0:T(8,128)} reshape(f32[32,32,2,768]{3,2,1,0:T(2,128)} %copy.154) | data formatting | bytes 12582912 | tf_op jit(solution)/shard_map/reshape | solution.py:247
  728.8 8.7 %gather_fusion.2 = f32[1024,768]{1,0:T(8,128)} fusion(f32[2048,768]{1,0:T(8,128)} %reshape.321, s32[1024]{0:T(1024)S(1)} %copy-done.14), kind=kCustom, calls=%fused_computation.2 | custom fusion | bytes 6295552 | tf_op jit(solution)/shard_map/gather | solution.py:247
  737.5 3.1 reshape.322
  740.6 2.9 reduce_sum.65
  (226 shorter events, 94.5 us)
Async XLA Ops:
  2.4 1.9 copy-start.1
  9.5 0.8 copy-start.16
  10.2 16.1 %copy-start.7 = (bf16[256,768]{1,0:T(8,128)(2,1)S(1)}, bf16[256,768]{1,0:T(8,128)(2,1)}, u32[]{:S(2)}) copy-start(bf16[256,768]{1,0:T(8,128)(2,1)} %param.9) | copy-start | bytes 1179652
  10.9 17.1 %copy-start.15 = (s32[1024,1]{0,1:T(1,128)}, s32[1024,1]{0,1:T(1,128)S(1)}, u32[]{:S(2)}) copy-start(s32[1024,1]{0,1:T(1,128)S(1)} %compare_select_fusion.1) | copy-start | bytes 12292
  16.7 28.0 %all-to-all-start = ((s32[32,1,576]{2,1,0:T(1,128)}), s32[32,1,576]{2,1,0:T(1,128)S(1)}, u32[]{:S(2)}, u32[]{:S(2)}) async-start(s32[32,1,576]{2,1,0:T(1,128)} %reshape.393), calls=%async_computation | async-start | bytes 163840 | tf_op jit(solution)/shard_map/all_to_all | solution.py:181
  44.7 7.4 copy-start.8
  44.7 47.1 %all-to-all-start.1 = ((bf16[32,32,2,768]{3,2,0,1:T(2,128)(2,1)}), bf16[32,32,2,768]{3,2,0,1:T(2,128)(2,1)S(1)}, u32[]{:S(2)}, u32[]{:S(2)}) async-start(bf16[32,32,2,768]{3,2,0,1:T(2,128)(2,1)} %copy.136), calls=%async_computation.1 | async-start | bytes 6291456 | tf_op jit(solution)/shard_map/all_to_all | solution.py:174
  58.8 0.7 copy-start.3
  112.8 9.4 %copy-start = (bf16[8,64,96,16]{1,3,2,0:T(8,128)(2,1)S(1)}, bf16[8,64,96,16]{1,3,2,0:T(8,128)(2,1)}, u32[]{:S(2)}) copy-start(bf16[8,64,96,16]{1,3,2,0:T(8,128)(2,1)} %copy.181) | copy-start | bytes 4718596 | tf_op jit(solution)/shard_map/while
  145.2 9.4 %copy-start = (bf16[8,64,96,16]{1,3,2,0:T(8,128)(2,1)S(1)}, bf16[8,64,96,16]{1,3,2,0:T(8,128)(2,1)}, u32[]{:S(2)}) copy-start(bf16[8,64,96,16]{1,3,2,0:T(8,128)(2,1)} %copy.181) | copy-start | bytes 4718596 | tf_op jit(solution)/shard_map/while
  177.6 9.4 %copy-start = (bf16[8,64,96,16]{1,3,2,0:T(8,128)(2,1)S(1)}, bf16[8,64,96,16]{1,3,2,0:T(8,128)(2,1)}, u32[]{:S(2)}) copy-start(bf16[8,64,96,16]{1,3,2,0:T(8,128)(2,1)} %copy.181) | copy-start | bytes 4718596 | tf_op jit(solution)/shard_map/while
  210.0 9.4 %copy-start = (bf16[8,64,96,16]{1,3,2,0:T(8,128)(2,1)S(1)}, bf16[8,64,96,16]{1,3,2,0:T(8,128)(2,1)}, u32[]{:S(2)}) copy-start(bf16[8,64,96,16]{1,3,2,0:T(8,128)(2,1)} %copy.181) | copy-start | bytes 4718596 | tf_op jit(solution)/shard_map/while
  247.1 12.3 %all-to-all-start.4 = ((f32[32,32,2]{0,2,1:T(2,128)}), f32[32,32,2]{0,2,1:T(2,128)S(1)}, u32[]{:S(2)}, u32[]{:S(2)}) async-start(f32[32,32,2]{0,2,1:T(2,128)} %get-tuple-element.255), calls=%async_computation.4 | async-start | bytes 65536 | tf_op jit(solution)/shard_map/all_to_all | solution.py:203
  252.2 14.2 %copy-start.13 = (s32[1024]{0:T(1024)}, s32[1024]{0:T(1024)S(1)}, u32[]{:S(2)}) copy-start(s32[1024]{0:T(1024)S(1)} %broadcast_clamp_fusion) | copy-start | bytes 12292
  259.4 34.5 %copy-start.4 = (s32[32,32,2,9]{0,2,1,3:T(2,128)S(1)}, s32[32,32,2,9]{0,2,1,3:T(2,128)}, u32[]{:S(2)}) copy-start(s32[32,32,2,9]{0,2,1,3:T(2,128)} %copy-done.3) | copy-start | bytes 221188
  272.8 14.8 %all-to-all-start.5 = ((f32[32,32,2]{0,2,1:T(2,128)}), f32[32,32,2]{0,2,1:T(2,128)S(1)}, u32[]{:S(2)}, u32[]{:S(2)}) async-start(f32[32,32,2]{0,2,1:T(2,128)} %copy.148), calls=%async_computation.5 | async-start | bytes 65536 | tf_op jit(solution)/shard_map/all_to_all | solution.py:225
  287.6 13.5 %all-to-all-start.3 = ((f32[32,32,2]{0,2,1:T(2,128)}), f32[32,32,2]{0,2,1:T(2,128)S(1)}, u32[]{:S(2)}, u32[]{:S(2)}) async-start(f32[32,32,2]{0,2,1:T(2,128)} %copy.144), calls=%async_computation.3 | async-start | bytes 65536 | tf_op jit(solution)/shard_map/all_to_all | solution.py:218
  301.5 0.6 copy-start.9
  301.5 0.6 copy-start.11
  301.5 8.5 %copy-start.5 = (s32[4,8,64,9]{2,1,3,0:T(8,128)}, s32[4,8,64,9]{2,1,3,0:T(8,128)S(1)}, u32[]{:S(2)}) copy-start(s32[4,8,64,9]{2,1,3,0:T(8,128)S(1)} %get-tuple-element.429) | copy-start | bytes 221188 | tf_op jit(solution)/shard_map/while
  346.3 8.3 %copy-start.6 = (s32[4,8,64,9]{2,1,3,0:T(8,128)S(1)}, s32[4,8,64,9]{2,1,3,0:T(8,128)}, u32[]{:S(2)}) copy-start(s32[4,8,64,9]{2,1,3,0:T(8,128)} %copy-done.5) | copy-start | bytes 221188 | tf_op jit(solution)/shard_map/while
  346.3 8.3 %copy-start.10 = (f32[4,8,64]{2,1,0:T(8,128)S(1)}, f32[4,8,64]{2,1,0:T(8,128)}, u32[]{:S(2)}) copy-start(f32[4,8,64]{2,1,0:T(8,128)} %copy-done.9) | copy-start | bytes 24580 | tf_op jit(solution)/shard_map/while
  346.3 8.3 %copy-start.12 = (f32[4,8,64]{2,1,0:T(8,128)S(1)}, f32[4,8,64]{2,1,0:T(8,128)}, u32[]{:S(2)}) copy-start(f32[4,8,64]{2,1,0:T(8,128)} %copy-done.11) | copy-start | bytes 24580 | tf_op jit(solution)/shard_map/while
  354.6 0.6 copy-start.9
  354.6 0.6 copy-start.11
  354.6 8.5 %copy-start.5 = (s32[4,8,64,9]{2,1,3,0:T(8,128)}, s32[4,8,64,9]{2,1,3,0:T(8,128)S(1)}, u32[]{:S(2)}) copy-start(s32[4,8,64,9]{2,1,3,0:T(8,128)S(1)} %get-tuple-element.429) | copy-start | bytes 221188 | tf_op jit(solution)/shard_map/while
  399.4 8.2 %copy-start.6 = (s32[4,8,64,9]{2,1,3,0:T(8,128)S(1)}, s32[4,8,64,9]{2,1,3,0:T(8,128)}, u32[]{:S(2)}) copy-start(s32[4,8,64,9]{2,1,3,0:T(8,128)} %copy-done.5) | copy-start | bytes 221188 | tf_op jit(solution)/shard_map/while
  399.4 8.2 %copy-start.10 = (f32[4,8,64]{2,1,0:T(8,128)S(1)}, f32[4,8,64]{2,1,0:T(8,128)}, u32[]{:S(2)}) copy-start(f32[4,8,64]{2,1,0:T(8,128)} %copy-done.9) | copy-start | bytes 24580 | tf_op jit(solution)/shard_map/while
  399.4 8.2 %copy-start.12 = (f32[4,8,64]{2,1,0:T(8,128)S(1)}, f32[4,8,64]{2,1,0:T(8,128)}, u32[]{:S(2)}) copy-start(f32[4,8,64]{2,1,0:T(8,128)} %copy-done.11) | copy-start | bytes 24580 | tf_op jit(solution)/shard_map/while
  407.7 0.6 copy-start.9
  407.7 0.6 copy-start.11
  407.7 8.5 %copy-start.5 = (s32[4,8,64,9]{2,1,3,0:T(8,128)}, s32[4,8,64,9]{2,1,3,0:T(8,128)S(1)}, u32[]{:S(2)}) copy-start(s32[4,8,64,9]{2,1,3,0:T(8,128)S(1)} %get-tuple-element.429) | copy-start | bytes 221188 | tf_op jit(solution)/shard_map/while
  452.5 8.3 %copy-start.6 = (s32[4,8,64,9]{2,1,3,0:T(8,128)S(1)}, s32[4,8,64,9]{2,1,3,0:T(8,128)}, u32[]{:S(2)}) copy-start(s32[4,8,64,9]{2,1,3,0:T(8,128)} %copy-done.5) | copy-start | bytes 221188 | tf_op jit(solution)/shard_map/while
  452.5 8.3 %copy-start.10 = (f32[4,8,64]{2,1,0:T(8,128)S(1)}, f32[4,8,64]{2,1,0:T(8,128)}, u32[]{:S(2)}) copy-start(f32[4,8,64]{2,1,0:T(8,128)} %copy-done.9) | copy-start | bytes 24580 | tf_op jit(solution)/shard_map/while
  452.5 8.3 %copy-start.12 = (f32[4,8,64]{2,1,0:T(8,128)S(1)}, f32[4,8,64]{2,1,0:T(8,128)}, u32[]{:S(2)}) copy-start(f32[4,8,64]{2,1,0:T(8,128)} %copy-done.11) | copy-start | bytes 24580 | tf_op jit(solution)/shard_map/while
  460.7 0.6 copy-start.9
  460.8 0.6 copy-start.11
  460.8 8.5 %copy-start.5 = (s32[4,8,64,9]{2,1,3,0:T(8,128)}, s32[4,8,64,9]{2,1,3,0:T(8,128)S(1)}, u32[]{:S(2)}) copy-start(s32[4,8,64,9]{2,1,3,0:T(8,128)S(1)} %get-tuple-element.429) | copy-start | bytes 221188 | tf_op jit(solution)/shard_map/while
  505.6 8.2 %copy-start.6 = (s32[4,8,64,9]{2,1,3,0:T(8,128)S(1)}, s32[4,8,64,9]{2,1,3,0:T(8,128)}, u32[]{:S(2)}) copy-start(s32[4,8,64,9]{2,1,3,0:T(8,128)} %copy-done.5) | copy-start | bytes 221188 | tf_op jit(solution)/shard_map/while
  505.6 8.2 %copy-start.10 = (f32[4,8,64]{2,1,0:T(8,128)S(1)}, f32[4,8,64]{2,1,0:T(8,128)}, u32[]{:S(2)}) copy-start(f32[4,8,64]{2,1,0:T(8,128)} %copy-done.9) | copy-start | bytes 24580 | tf_op jit(solution)/shard_map/while
  505.6 8.2 %copy-start.12 = (f32[4,8,64]{2,1,0:T(8,128)S(1)}, f32[4,8,64]{2,1,0:T(8,128)}, u32[]{:S(2)}) copy-start(f32[4,8,64]{2,1,0:T(8,128)} %copy-done.11) | copy-start | bytes 24580 | tf_op jit(solution)/shard_map/while
  514.0 5.0 copy-start.2
  514.1 195.9 %all-to-all-start.6 = ((f32[32,32,2,768]{3,0,2,1:T(8,128)}), f32[32,32,2,768]{3,0,2,1:T(8,128)}, u32[]{:S(2)}, u32[]{:S(2)}) async-start(f32[32,32,2,768]{3,0,2,1:T(8,128)} %bitcast.170), calls=%async_computation.6 | async-start | bytes 12582912 | tf_op jit(solution)/shard_map/all_to_all | solution.py:240
  720.3 8.5 %copy-start.14 = (s32[1024]{0:T(1024)S(1)}, s32[1024]{0:T(1024)}, u32[]{:S(2)}) copy-start(s32[1024]{0:T(1024)} %copy-done.13) | copy-start | bytes 12292
